TPU v7x, 32 devices: a whole 2x2x4 slice. The times are simulated.
32 devices in a mesh: dp: 8 (over z, y), mp: 4 (over x, core).
Axes of the slice: x: 2, y: 2, z: 4, core: 2. Of those that a mesh axis runs over, the one named last changes fastest.
Arguments:
- tokens: bfloat16 [16384, 1024], P(('dp', 'mp')), may hold values from -6 to 6
- segment_ids: int32 [16384], P(('dp', 'mp')), may hold values from 0 to 63, never falling along the last dimension, each value on 1 to 512 neighbouring positions
- w_qkv: bfloat16 [3, 1024, 1024], P(None, None, 'mp'), may hold values from -0.1875 to 0.1875
- b_qv: bfloat16 [2, 1024], P(None, 'mp'), may hold values from -1.75 to 1.75
- w_out: bfloat16 [1024, 1024], P('mp'), may hold values from -2 to 2
- b_out: bfloat16 [1024], replicated, may hold values from -1.75 to 1.75
- w_up: bfloat16 [1024, 4096], P(None, 'mp'), may hold values from -0.1875 to 0.1875
- b_up: bfloat16 [4096], P('mp'), may hold values from -1.75 to 1.75
- w_down: bfloat16 [4096, 1024], P('mp'), may hold values from -0.125 to 0.125
- b_down: bfloat16 [1024], replicated, may hold values from -1.75 to 1.75
- ln_gain: float32 [2, 1024], replicated, may hold values from 0.5 to 1.5
- ln_bias: float32 [2, 1024], replicated, may hold values from -1.75 to 1.75
- out_grad: bfloat16 [16384, 1024], P(('dp', 'mp')), may hold values from -6 to 6
Outputs:
- block_out: bfloat16 [16384, 1024], P(('dp', 'mp'))
- grad_in: float32 [16384, 1024], P(('dp', 'mp'))
- grad_qkv: float32 [3, 1024, 1024], P(None, None, 'mp')
- grad_bqv: float32 [2, 1024], P(None, 'mp')
- grad_wout: float32 [1024, 1024], P('mp')
- grad_bout: float32 [1024], replicated
- grad_up: float32 [1024, 4096], P(None, 'mp')
- grad_bup: float32 [4096], P('mp')
- grad_down: float32 [4096, 1024], P('mp')
- grad_bdown: float32 [1024], replicated
- grad_gain: float32 [2, 1024], replicated
- grad_shift: float32 [2, 1024], replicated
Inputs may be any that keep to these rules, and one draw needn't show every extreme that they name: `segment_ids`: along all frames in order, segment numbers never fall; each segment covers 1 to 512 frames and one covers exactly 512; attention never crosses a row of 1024 frames.
All inputs are finite; a program needn't handle non-finite values.
Results may differ from a plain program's by a relative error of at most 0.02.
Values may be sent and summed in bfloat16 or wider, within the bound.
No kernel may reach another device: no remote copies, remote signals or barrier semaphores. Data moves between devices by JAX's collectives and lax.ppermute only.
A program may use at most 192 MiB of HBM per device.

v0:
```python
import jax
import jax.numpy as jnp
from jax import lax
from jax.sharding import PartitionSpec as P

HD = 64
LEN = 1024
QBLK = 512
EPS = 1e-05


def norm_rows(values, gain, shift):
    center = values - jnp.mean(values, axis=-1, keepdims=True)
    spread = jnp.mean(center * center, axis=-1, keepdims=True)
    return center * lax.rsqrt(spread + EPS) * gain + shift


def split_heads(flat, rows):
    return flat.reshape(rows, LEN, flat.shape[1] // HD, HD)


def block_scores(query, keys, seg_q, seg_k, offset):
    scores = jnp.einsum(
        "rqhd,rkhd->rhqk", query, keys, preferred_element_type=jnp.float32
    ) * HD ** (-0.5)
    q_pos = offset + jnp.arange(query.shape[1], dtype=jnp.int32)
    k_pos = jnp.arange(keys.shape[1], dtype=jnp.int32)
    allowed = (seg_q[:, :, None] == seg_k[:, None, :]) & (
        k_pos[None, None, :] <= q_pos[None, :, None]
    )
    return jnp.where(allowed[:, None], scores, -1e30)


def attention_forward(query, keys, values, seg_all):
    rows = query.shape[0] // LEN
    q4 = split_heads(query, rows)
    k4 = split_heads(keys, rows)
    v4 = split_heads(values, rows)
    seg2 = seg_all.reshape(rows, LEN)
    outputs = []
    totals = []
    for block in range(LEN // QBLK):
        first = block * QBLK
        end = first + QBLK
        scores = block_scores(
            q4[:, first:end], k4[:, :end], seg2[:, first:end], seg2[:, :end], first
        )
        top = jnp.max(scores, axis=-1, keepdims=True)
        expd = jnp.exp(scores - top)
        summed = jnp.sum(expd, axis=-1, keepdims=True)
        weights = (expd / summed).astype(jnp.bfloat16)
        outputs.append(
            jnp.einsum("rhqk,rkhd->rqhd", weights, v4[:, :end], preferred_element_type=jnp.float32)
        )
        totals.append(top + jnp.log(summed))
    attended = jnp.concatenate(outputs, axis=1).reshape(query.shape).astype(jnp.bfloat16)
    return (attended, totals)


def attention_backward(query, keys, values, seg_all, totals, grad_att):
    rows = query.shape[0] // LEN
    q4 = split_heads(query, rows)
    k4 = split_heads(keys, rows)
    v4 = split_heads(values, rows)
    g4 = split_heads(grad_att, rows)
    seg2 = seg_all.reshape(rows, LEN)
    scale = HD ** (-0.5)
    grad_k = jnp.zeros(k4.shape, jnp.float32)
    grad_v = jnp.zeros(v4.shape, jnp.float32)
    grad_q_parts = []
    for block in range(LEN // QBLK):
        first = block * QBLK
        end = first + QBLK
        scores = block_scores(
            q4[:, first:end], k4[:, :end], seg2[:, first:end], seg2[:, :end], first
        )
        probs = jnp.exp(scores - totals[block])
        weights = probs.astype(jnp.bfloat16)
        grad_w = jnp.einsum(
            "rqhd,rkhd->rhqk", g4[:, first:end], v4[:, :end], preferred_element_type=jnp.float32
        )
        delta = jnp.sum(probs * grad_w, axis=-1, keepdims=True)
        grad_s = (probs * (grad_w - delta)).astype(jnp.bfloat16)
        grad_q_parts.append(
            jnp.einsum("rhqk,rkhd->rqhd", grad_s, k4[:, :end], preferred_element_type=jnp.float32)
            * scale
        )
        padding = ((0, 0), (0, LEN - end), (0, 0), (0, 0))
        grad_k = grad_k + jnp.pad(
            jnp.einsum(
                "rhqk,rqhd->rkhd", grad_s, q4[:, first:end], preferred_element_type=jnp.float32
            )
            * scale,
            padding,
        )
        grad_v = grad_v + jnp.pad(
            jnp.einsum(
                "rhqk,rqhd->rkhd", weights, g4[:, first:end], preferred_element_type=jnp.float32
            ),
            padding,
        )
    shape = query.shape
    grad_q = jnp.concatenate(grad_q_parts, axis=1).reshape(shape).astype(jnp.bfloat16)
    return (
        grad_q,
        grad_k.reshape(shape).astype(jnp.bfloat16),
        grad_v.reshape(shape).astype(jnp.bfloat16),
    )


def shards(
    tokens,
    segment_ids,
    w_qkv,
    b_qv,
    w_out,
    b_out,
    w_up,
    b_up,
    w_down,
    b_down,
    ln_gain,
    ln_bias,
    out_grad,
):
    resid = tokens.astype(jnp.float32)
    qv_bias = b_qv.astype(jnp.float32)
    up_bias = b_up.astype(jnp.float32)
    local_rows = tokens.shape[0]
    normed, first_back = jax.vjp(norm_rows, resid, ln_gain[0], ln_bias[0])
    lowered = normed.astype(jnp.bfloat16)
    joined, seg_all = (
        lax.all_gather(lowered, "mp", axis=0, tiled=True),
        lax.all_gather(segment_ids, "mp", axis=0, tiled=True),
    )
    query = (jnp.dot(joined, w_qkv[0], preferred_element_type=jnp.float32) + qv_bias[0]).astype(
        jnp.bfloat16
    )
    keys = jnp.dot(joined, w_qkv[1], preferred_element_type=jnp.float32).astype(jnp.bfloat16)
    values = (jnp.dot(joined, w_qkv[2], preferred_element_type=jnp.float32) + qv_bias[1]).astype(
        jnp.bfloat16
    )
    query, keys, values = (query, keys, values)
    attended, totals = attention_forward(query, keys, values, seg_all)
    attn_sum = lax.psum_scatter(
        jnp.dot(attended, w_out, preferred_element_type=jnp.float32).astype(jnp.bfloat16),
        "mp",
        scatter_dimension=0,
        tiled=True,
    ).astype(jnp.float32)
    mixed = resid + attn_sum + b_out.astype(jnp.float32)
    normed2, second_back = jax.vjp(norm_rows, mixed, ln_gain[1], ln_bias[1])
    lowered2 = normed2.astype(jnp.bfloat16)
    joined2 = lax.all_gather(lowered2, "mp", axis=0, tiled=True)
    pre_act = jnp.dot(joined2, w_up, preferred_element_type=jnp.float32) + up_bias
    pre_act, activ = (pre_act, jax.nn.gelu(pre_act, approximate=False).astype(jnp.bfloat16))
    block_out = (
        mixed
        + lax.psum_scatter(
            jnp.dot(activ, w_down, preferred_element_type=jnp.float32).astype(jnp.bfloat16),
            "mp",
            scatter_dimension=0,
            tiled=True,
        ).astype(jnp.float32)
        + b_down.astype(jnp.float32)
    ).astype(jnp.bfloat16)
    grad_y = out_grad.astype(jnp.float32)
    grad_z = lax.all_gather(out_grad, "mp", axis=0, tiled=True)
    grad_down = jnp.einsum("tf,td->fd", activ, grad_z, preferred_element_type=jnp.float32)
    grad_bdown = jnp.sum(grad_z, axis=0, dtype=jnp.float32)
    grad_act = jnp.einsum("td,fd->tf", grad_z, w_down, preferred_element_type=jnp.float32)
    gelu_back = jax.vjp(lambda value: jax.nn.gelu(value, approximate=False), pre_act)[1]
    grad_pre = gelu_back(grad_act)[0].astype(jnp.bfloat16)
    grad_up = jnp.einsum("td,tf->df", joined2, grad_pre, preferred_element_type=jnp.float32)
    grad_bup = jnp.sum(grad_pre, axis=0, dtype=jnp.float32)
    grad_n2 = lax.psum_scatter(
        jnp.einsum("tf,df->td", grad_pre, w_up, preferred_element_type=jnp.float32).astype(
            jnp.bfloat16
        ),
        "mp",
        scatter_dimension=0,
        tiled=True,
    ).astype(jnp.float32)
    grad_h, grad_g2, grad_s2 = second_back(grad_n2)
    grad_h = grad_h + grad_y
    grad_branch = lax.all_gather(grad_h.astype(jnp.bfloat16), "mp", axis=0, tiled=True)
    grad_wout = jnp.einsum("tc,td->cd", attended, grad_branch, preferred_element_type=jnp.float32)
    grad_bout = jnp.sum(grad_branch, axis=0, dtype=jnp.float32)
    grad_att = jnp.einsum(
        "td,cd->tc", grad_branch, w_out, preferred_element_type=jnp.float32
    ).astype(jnp.bfloat16)
    grad_q, grad_k, grad_v = attention_backward(query, keys, values, seg_all, totals, grad_att)
    grad_qkv = jnp.stack(
        [
            jnp.einsum("td,tc->dc", joined, piece, preferred_element_type=jnp.float32)
            for piece in (grad_q, grad_k, grad_v)
        ]
    )
    grad_bqv = jnp.stack(
        [jnp.sum(grad_q, axis=0, dtype=jnp.float32), jnp.sum(grad_v, axis=0, dtype=jnp.float32)]
    )
    summed = jnp.zeros((local_rows * lax.axis_size("mp"), w_qkv.shape[1]), jnp.float32)
    for index, piece in enumerate((grad_q, grad_k, grad_v)):
        summed = summed + jnp.einsum(
            "tc,dc->td", piece, w_qkv[index], preferred_element_type=jnp.float32
        )
    grad_n1 = lax.psum_scatter(
        summed.astype(jnp.bfloat16), "mp", scatter_dimension=0, tiled=True
    ).astype(jnp.float32)
    grad_x, grad_g1, grad_s1 = first_back(grad_n1)
    grad_in = grad_x + grad_h
    weight_totals = (
        lax.psum(grad_qkv.astype(jnp.bfloat16), "dp").astype(jnp.float32),
        lax.psum(grad_bqv.astype(jnp.bfloat16), "dp").astype(jnp.float32),
        lax.psum(grad_wout.astype(jnp.bfloat16), "dp").astype(jnp.float32),
        lax.psum(grad_bout.astype(jnp.bfloat16), "dp").astype(jnp.float32),
        lax.psum(grad_up.astype(jnp.bfloat16), "dp").astype(jnp.float32),
        lax.psum(grad_bup.astype(jnp.bfloat16), "dp").astype(jnp.float32),
        lax.psum(grad_down.astype(jnp.bfloat16), "dp").astype(jnp.float32),
        lax.psum(grad_bdown.astype(jnp.bfloat16), "dp").astype(jnp.float32),
    )
    norm_totals = lax.psum(
        (jnp.stack([grad_g1, grad_g2]), jnp.stack([grad_s1, grad_s2])), ("dp", "mp")
    )
    return (block_out, grad_in) + tuple(weight_totals) + tuple(norm_totals)


def solution(mesh):
    in_specs = (
        P(("dp", "mp"), None),
        P(("dp", "mp")),
        P(None, None, "mp"),
        P(None, "mp"),
        P("mp", None),
        P(),
        P(None, "mp"),
        P("mp"),
        P("mp", None),
        P(),
        P(),
        P(),
        P(("dp", "mp"), None),
    )
    out_specs = (
        P(("dp", "mp"), None),
        P(("dp", "mp"), None),
        P(None, None, "mp"),
        P(None, "mp"),
        P("mp", None),
        P(),
        P(None, "mp"),
        P("mp"),
        P("mp", None),
        P(),
        P(),
        P(),
    )
    return jax.shard_map(shards, mesh=mesh, in_specs=in_specs, out_specs=out_specs, check_vma=False)
```

profile of v0, /device:TPU:0, one launch (start us, length us, event | category | flops | bytes accessed | tf_op | source)
XLA Modules:
  0.0 795.8 jit_solution(3557118762227939732)
XLA Ops:
  15.4 6.2 all-gather
  25.2 27.5 %all-gather.6.cloned.1.call-done = bf16[2048,1024]{1,0:T(8,128)(2,1)} async-done(((bf16[512,1024]{1,0:T(8,128)(2,1)}), bf16[2048,1024]{1,0:T(8,128)(2,1)}) %all-gather.6.cloned.1.call-update) | async-done | bytes 4194320 | tf_op jit(solution)/shard_map/all_gather | solution.py:133
  52.7 3.6 fusion.22
  58.2 4.0 copy.62
  62.3 3.6 fusion.23
  100.2 4.0 fusion.55
  110.7 44.1 %reduce-scatter.5.cloned.1.call-done = bf16[512,1024]{1,0:T(8,128)(2,1)} async-done(((bf16[2048,1024]{1,0:T(8,128)(2,1)}), bf16[512,1024]{1,0:T(8,128)(2,1)}) %reduce-scatter.5.cloned.1.call-update) | async-done | bytes 1048592 | tf_op jit(solution)/shard_map/reduce_scatter | solution.py:145
  160.6 34.0 %all-gather.8.cloned.1.call-done = bf16[2048,1024]{1,0:T(8,128)(2,1)} async-done(((bf16[512,1024]{1,0:T(8,128)(2,1)}), bf16[2048,1024]{1,0:T(8,128)(2,1)}) %all-gather.8.cloned.1.call-update) | async-done | bytes 4194320 | tf_op jit(solution)/shard_map/all_gather | solution.py:154
  194.6 11.3 %fusion.91 = f32[2048,1024]{1,0:T(8,128)} fusion(bf16[2048,1024]{1,0:T(8,128)(2,1)} %all-gather.8.cloned.1.call-done, bf16[1024,1024]{1,0:T(8,128)(2,1)} %param.19), kind=kOutput, calls=%fused_computation.163 | convolution fusion | flops 4294967296 | bytes 14680064 | tf_op jit(solution)/shard_map/dot_general | solution.py:155
  205.9 24.6 %all-gather.10.cloned.1.call-done = bf16[2048,1024]{1,0:T(8,128)(2,1)} async-done(((bf16[512,1024]{1,0:T(8,128)(2,1)}), bf16[2048,1024]{1,0:T(8,128)(2,1)}) %all-gather.10.cloned.1.call-update) | async-done | bytes 4194320 | tf_op jit(solution)/shard_map/all_gather | solution.py:168
  230.5 27.5 %fusion.78 = (bf16[1024]{0:T(1024)(128)(2,1)S(1)}, bf16[2048,1024]{1,0:T(8,128)(2,1)S(1)}, f32[2048,1024]{1,0:T(8,128)}) fusion(f32[2048,1024]{1,0:T(8,128)} %fusion.91, f32[1024]{0:T(1024)S(1)} %convert_element_type.188, bf16[2048,1024]{1,0:T(8,128)(2,1)} %all-gather.10.cloned.1.call-done, bf16[1024,1024]{1,0:T(8,128)(2,1)S(1)} %copy-done), kind=kOutput, calls=%fused_computation.151 | convolution fusion | flops 4450155520 | bytes 27269120 | tf_op jit(solution)/shard_map/td,fd->tf/dot_general | solution.py:171
  260.0 6.2 convolution_convert_fusion.1
  266.3 10.4 %multiply_convert_fusion.2 = bf16[2048,1024]{1,0:T(8,128)(2,1)} fusion(f32[2048,1024]{1,0:T(8,128)} %get-tuple-element.31, f32[2048,1024]{1,0:T(8,128)} %fusion.91, f32[1024]{0:T(1024)S(1)} %convert_element_type.188), kind=kLoop, calls=%fused_computation.17 | loop fusion | flops 8388608 | bytes 20975616 | tf_op jit(solution)/shard_map/convert_element_type | solution.py:156
  276.7 8.4 %convolution_convert_fusion.2 = bf16[2048,1024]{1,0:T(8,128)(2,1)} fusion(bf16[2048,1024]{1,0:T(8,128)(2,1)} %multiply_convert_fusion.2, bf16[1024,1024]{1,0:T(8,128)(2,1)S(1)} %copy-done), kind=kOutput, calls=%fused_computation.43 | convolution fusion | flops 4297064448 | bytes 10485760 | tf_op jit(solution)/shard_map/dot_general | solution.py:160
  285.7 25.2 %reduce-scatter.9.cloned.1.call-done = bf16[512,1024]{1,0:T(8,128)(2,1)} async-done(((bf16[2048,1024]{1,0:T(8,128)(2,1)}), bf16[512,1024]{1,0:T(8,128)(2,1)}) %reduce-scatter.9.cloned.1.call-update) | async-done | bytes 1048592 | tf_op jit(solution)/shard_map/reduce_scatter | solution.py:176
  313.3 44.7 %reduce-scatter.7.cloned.1.call-done = bf16[512,1024]{1,0:T(8,128)(2,1)} async-done(((bf16[2048,1024]{1,0:T(8,128)(2,1)}), bf16[512,1024]{1,0:T(8,128)(2,1)}) %reduce-scatter.7.cloned.1.call-update) | async-done | bytes 1048592 | tf_op jit(solution)/shard_map/reduce_scatter | solution.py:159
  358.0 3.7 fusion.81
  364.5 9.5 %convolution_convert_fusion.6 = bf16[1024,1024]{1,0:T(8,128)(2,1)} fusion(bf16[2048,1024]{1,0:T(8,128)(2,1)} %all-gather.8.cloned.1.call-done, bf16[2048,1024]{1,0:T(8,128)(2,1)} %copy-done.55), kind=kOutput, calls=%fused_computation.90 | convolution fusion | flops 4296015872 | bytes 10485760 | tf_op jit(solution)/shard_map/td,tf->df/dot_general | solution.py:174
  374.0 6.0 convolution_convert_fusion.5
  379.9 19.0 %all-gather.12.cloned.1.call-done = bf16[2048,1024]{1,0:T(8,128)(2,1)} async-done(((bf16[512,1024]{1,0:T(8,128)(2,1)}), bf16[2048,1024]{1,0:T(8,128)(2,1)}) %all-gather.12.cloned.1.call-update) | async-done | bytes 4194320 | tf_op jit(solution)/shard_map/all_gather | solution.py:186
  398.9 4.5 convolution_convert_fusion.3
  410.4 5.9 fusion.42
  416.3 4.6 multiply_reduce_fusion.1
  429.7 14.7 %multiply_reduce_fusion = (f32[2,4,512]{2,1,0:T(4,128)S(1)}, f32[2,4,512,1024]{3,2,1,0:T(8,128)}) fusion(f32[2,4,512,1024]{3,2,1,0:T(8,128)} %copy-done.2, f32[2,4,512]{2,1,0:T(4,128)S(1)} %bitcast.140, bf16[2,512,4,64]{1,3,2,0:T(8,128)(2,1)} %copy.98, bf16[2,1024,4,64]{1,3,2,0:T(8,128)(2,1)S(1)} %copy-done.15), kind=kOutput, calls=%fused_computation.1 | convolution fusion | flops 549449728 | bytes 35160064 | tf_op jit(solution)/shard_map/rqhd,rkhd->rhqk/dot_general | solution.py:79
  444.4 7.8 fusion.90
  453.6 10.9 %multiply_convert_fusion = bf16[2,4,512,1024]{3,2,1,0:T(8,128)(2,1)} fusion(f32[2,4,512,1024]{3,2,1,0:T(8,128)} %get-tuple-element.54, f32[2,4,512,1024]{3,2,1,0:T(8,128)S(1)} %bitcast.125, f32[2,4,512]{2,1,0:T(4,128)S(1)} %get-tuple-element.53, f32[2,4,512]{2,1,0:T(4,128)S(1)} %bitcast.142), kind=kLoop, calls=%fused_computation | loop fusion | flops 16777216 | bytes 41975808 | tf_op jit(solution)/shard_map/convert_element_type | solution.py:83
  464.6 6.2 fusion.47
  497.5 23.2 %all-reduce.3 = (bf16[2,256]{1,0:T(2,128)(2,1)S(1)}, bf16[1024]{0:T(1024)(128)(2,1)S(1)}, bf16[1024]{0:T(1024)(128)(2,1)S(1)}, bf16[1024]{0:T(1024)(128)(2,1)S(1)}) all-reduce(bf16[2,256]{1,0:T(2,128)(2,1)S(1)} %pad_maximum_fusion.4, bf16[1024]{0:T(1024)(128)(2,1)S(1)} %reduce_sum.244, ...), channel_id=1, replica_groups=mesh['dp'=8,'mp'=4] {'dp'}, use_global_device_ids=true, to_apply=%region_21.22 | all-reduce | flops 3584 | bytes 14336 | tf_op jit(solution)/shard_map/psum | solution.py:214
  523.1 171.2 %all-reduce.7.cloned.1.call-done = (bf16[3,1024,256]{2,1,0:T(8,128)(2,1)}, bf16[256,1024]{1,0:T(8,128)(2,1)}, bf16[1024,1024]{1,0:T(8,128)(2,1)}, bf16[1024,1024]{1,0:T(8,128)(2,1)}) async-done(((bf16[3,1024,256]{2,1,0:T(8,128)(2,1)}, bf16[256,1024]{1,0:T(8,128)(2,1)}, bf16[1024,1024]{1,0:T(8,128)(2,1)}, bf16[1024,1024]{1,0:T(8,128)(2,1)}), (bf16[3,1024,256]{2,1,0:T(8,128)(2,1)}, ...) | async-done | bytes 6291472 | tf_op jit(solution)/shard_map/psum | solution.py:213
  705.4 35.1 %reduce-scatter.11.cloned.1.call-done = bf16[512,1024]{1,0:T(8,128)(2,1)} async-done(((bf16[2048,1024]{1,0:T(8,128)(2,1)}), bf16[512,1024]{1,0:T(8,128)(2,1)}) %reduce-scatter.11.cloned.1.call-update) | async-done | bytes 1048592 | tf_op jit(solution)/shard_map/reduce_scatter | solution.py:207
  745.1 39.5 %all-reduce.2 = (f32[2,1024]{1,0:T(2,128)}, f32[2,1024]{1,0:T(2,128)}) all-reduce(f32[2,1024]{1,0:T(2,128)S(1)} %get-tuple-element.59, f32[2,1024]{1,0:T(2,128)S(1)} %get-tuple-element.60), channel_id=1, replica_groups=mesh['dp'=8,'mp'=4] {'dp','mp'}, use_global_device_ids=true, to_apply=%region_33.34 | all-reduce | flops 4096 | bytes 32768 | tf_op jit(solution)/shard_map/psum | solution.py:222
  784.5 4.5 add_add_fusion.2
  (232 shorter events, 129.4 us)
Async XLA Ops:
  7.2 223.3 %copy-start = (bf16[1024,1024]{1,0:T(8,128)(2,1)S(1)}, bf16[1024,1024]{1,0:T(8,128)(2,1)}, u32[]{:S(2)}) copy-start(bf16[1024,1024]{1,0:T(8,128)(2,1)} %param.21) | copy-start | bytes 6291460
  7.2 14.5 %copy-start.48 = (bf16[2,256]{1,0:T(2,128)(2,1)S(1)}, bf16[2,256]{1,0:T(2,128)(2,1)}, u32[]{:S(2)}) copy-start(bf16[2,256]{1,0:T(2,128)(2,1)} %param.16) | copy-start | bytes 3076
  7.2 45.5 %all-gather.6.cloned.1.call-start = ((), (), s32[]{:S(2)}) async-start(), calls=%async_computation.4 | async-start | bytes 5242880 | tf_op jit(solution)/shard_map/all_gather | solution.py:133
  8.8 12.9 %copy-start.40 = (f32[512]{0:T(512)}, f32[512]{0:T(512)S(1)}, u32[]{:S(2)}) copy-start(f32[512]{0:T(512)S(1)} %broadcast_multiply_fusion.1) | copy-start | bytes 6148
  11.9 9.9 %copy-start.38 = (f32[1,1024]{1,0:T(1,128)}, f32[1,1024]{1,0:T(1,128)S(1)}, u32[]{:S(2)}) copy-start(f32[1,1024]{1,0:T(1,128)S(1)} %get-tuple-element.43) | copy-start | bytes 12292
  15.3 139.4 %reduce-scatter.5.cloned.1.call-start = ((), (), s32[]{:S(2)}) async-start(), calls=%async_computation.5 | async-start | bytes 5242880 | tf_op jit(solution)/shard_map/reduce_scatter | solution.py:145
  110.0 44.8 %copy-start.4 = (bf16[512,1024]{1,0:T(8,128)(2,1)S(1)}, bf16[512,1024]{1,0:T(8,128)(2,1)}, u32[]{:S(2)}) copy-start(bf16[512,1024]{1,0:T(8,128)(2,1)} %param.13) | copy-start | bytes 3145732
  110.0 84.5 %all-gather.8.cloned.1.call-start = ((), (), s32[]{:S(2)}) async-start(), calls=%async_computation.6 | async-start | bytes 5242880 | tf_op jit(solution)/shard_map/all_gather | solution.py:154
  159.9 70.5 %all-gather.10.cloned.1.call-start = ((), (), s32[]{:S(2)}) async-start(), calls=%async_computation.8 | async-start | bytes 5242880 | tf_op jit(solution)/shard_map/all_gather | solution.py:168
  160.5 150.5 %reduce-scatter.9.cloned.1.call-start = ((), (), s32[]{:S(2)}) async-start(), calls=%async_computation.9 | async-start | bytes 5242880 | tf_op jit(solution)/shard_map/reduce_scatter | solution.py:176
  230.5 29.5 %copy-start.54 = (bf16[1024,1024]{1,0:T(8,128)(2,1)S(1)}, bf16[1024,1024]{1,0:T(8,128)(2,1)}, u32[]{:S(2)}) copy-start(bf16[1024,1024]{1,0:T(8,128)(2,1)} %param.19) | copy-start | bytes 6291460
  266.2 91.7 %reduce-scatter.7.cloned.1.call-start = ((), (), s32[]{:S(2)}) async-start(), calls=%async_computation.7 | async-start | bytes 5242880 | tf_op jit(solution)/shard_map/reduce_scatter | solution.py:159
  285.1 25.9 %copy-start.7 = (bf16[512,1024]{1,0:T(8,128)(2,1)S(1)}, bf16[512,1024]{1,0:T(8,128)(2,1)}, u32[]{:S(2)}) copy-start(bf16[512,1024]{1,0:T(8,128)(2,1)} %reduce-scatter.5.cloned.1.call-done) | copy-start | bytes 3145732
  285.1 113.9 %all-gather.12.cloned.1.call-start = ((), (), s32[]{:S(2)}) async-start(), calls=%async_computation.10 | async-start | bytes 5242880 | tf_op jit(solution)/shard_map/all_gather | solution.py:186
  313.3 49.7 %copy-start.11 = (bf16[512,1024]{1,0:T(8,128)(2,1)S(1)}, bf16[512,1024]{1,0:T(8,128)(2,1)}, u32[]{:S(2)}) copy-start(bf16[512,1024]{1,0:T(8,128)(2,1)} %param.25) | copy-start | bytes 3145732
  364.3 330.0 %all-reduce.7.cloned.1.call-start = ((), (), s32[]{:S(2)}) async-start(), calls=%async_computation.12 | async-start | bytes 12582912 | tf_op jit(solution)/shard_map/psum | solution.py:213
  364.4 9.5 %copy-start.26 = (bf16[2048,1024]{1,0:T(8,128)(2,1)S(1)}, bf16[2048,1024]{1,0:T(8,128)(2,1)}, u32[]{:S(2)}) copy-start(bf16[2048,1024]{1,0:T(8,128)(2,1)} %all-gather.10.cloned.1.call-done) | copy-start | bytes 12582916
  364.4 9.5 %copy-start.28 = (bf16[2048,1024]{1,0:T(8,128)(2,1)S(1)}, bf16[2048,1024]{1,0:T(8,128)(2,1)}, u32[]{:S(2)}) copy-start(bf16[2048,1024]{1,0:T(8,128)(2,1)} %multiply_convert_fusion.2) | copy-start | bytes 12582916
  374.0 25.0 %copy-start.35 = (bf16[256,1024]{1,0:T(8,128)(2,1)S(1)}, bf16[256,1024]{1,0:T(8,128)(2,1)}, u32[]{:S(2)}) copy-start(bf16[256,1024]{1,0:T(8,128)(2,1)} %param.17) | copy-start | bytes 1572868
  410.4 10.5 %slice-start.4 = ((s8[8388608]{0:T(1024)(128)(4,1)}), s8[4194304]{0:T(1024)(128)(4,1)S(1)}, s32[]{:S(2)}) async-start(s8[8388608]{0:T(1024)(128)(4,1)} %bitcast.126), calls=%async_computation.17 | async-start | bytes 8388608
  429.6 14.7 %copy-start.20 = (bf16[2,512,4,64]{1,3,2,0:T(8,128)(2,1)S(1)}, bf16[2,512,4,64]{1,3,2,0:T(8,128)(2,1)}, u32[]{:S(2)}) copy-start(bf16[2,512,4,64]{1,3,2,0:T(8,128)(2,1)} %copy.98) | copy-start | bytes 1572868
  429.6 14.7 %copy-start.22 = (f32[2,512,4,64]{1,3,2,0:T(8,128)S(1)}, f32[2,512,4,64]{1,3,2,0:T(8,128)}, u32[]{:S(2)}) copy-start(f32[2,512,4,64]{1,3,2,0:T(8,128)} %fusion.42) | copy-start | bytes 3145732
  429.6 23.9 %slice-start = ((s8[16777216]{0:T(1024)(128)(4,1)}), s8[4194304]{0:T(1024)(128)(4,1)S(1)}, s32[]{:S(2)}) async-start(s8[16777216]{0:T(1024)(128)(4,1)} %bitcast.124), calls=%async_computation.13 | async-start | bytes 8388608
  429.6 23.9 %slice-start.1 = ((s8[16777216]{0:T(1024)(128)(4,1)}), s8[4194304]{0:T(1024)(128)(4,1)S(1)}, s32[]{:S(2)}) async-start(s8[16777216]{0:T(1024)(128)(4,1)} %bitcast.124), calls=%async_computation.14 | async-start | bytes 8388608
  429.6 23.9 %slice-start.2 = ((s8[16777216]{0:T(1024)(128)(4,1)}), s8[4194304]{0:T(1024)(128)(4,1)S(1)}, s32[]{:S(2)}) async-start(s8[16777216]{0:T(1024)(128)(4,1)} %bitcast.124), calls=%async_computation.15 | async-start | bytes 8388608
  453.5 21.8 %copy-start.23 = (bf16[32,8,2,1024]{3,1,2,0:T(8,128)(2,1)}, bf16[32,8,2,1024]{3,1,2,0:T(8,128)(2,1)S(1)}, u32[]{:S(2)}) copy-start(bf16[32,8,2,1024]{3,1,2,0:T(8,128)(2,1)S(1)} %copy.102) | copy-start | bytes 3145732
  483.1 257.4 %reduce-scatter.11.cloned.1.call-start = ((), (), s32[]{:S(2)}) async-start(), calls=%async_computation.11 | async-start | bytes 5242880 | tf_op jit(solution)/shard_map/reduce_scatter | solution.py:207
  702.4 38.1 %copy-start.39 = (f32[1,1024]{1,0:T(1,128)S(1)}, f32[1,1024]{1,0:T(1,128)}, u32[]{:S(2)}) copy-start(f32[1,1024]{1,0:T(1,128)} %copy-done.38) | copy-start | bytes 12292
  702.4 38.1 %copy-start.41 = (f32[512]{0:T(512)S(1)}, f32[512]{0:T(512)}, u32[]{:S(2)}) copy-start(f32[512]{0:T(512)} %copy-done.40) | copy-start | bytes 6148
  702.4 40.0 %copy-start.47 = (f32[512]{0:T(512)S(1)}, f32[512]{0:T(512)}, u32[]{:S(2)}) copy-start(f32[512]{0:T(512)} %copy-done.46) | copy-start | bytes 6148
  702.4 40.0 %copy-start.45 = (f32[512]{0:T(512)S(1)}, f32[512]{0:T(512)}, u32[]{:S(2)}) copy-start(f32[512]{0:T(512)} %copy-done.44) | copy-start | bytes 6148
  742.5 46.6 %copy-start.1 = (bf16[1024,1024]{1,0:T(8,128)(2,1)S(1)}, bf16[1024,1024]{1,0:T(8,128)(2,1)}, u32[]{:S(2)}) copy-start(bf16[1024,1024]{1,0:T(8,128)(2,1)} %param.21) | copy-start | bytes 6291460
  (39 other events, 131.2 us)
Sparse Core Ops, SparseCore 0:
  15.5 37.1 all-gather.5
  110.2 44.5 reduce-scatter.4
  160.0 34.4 all-gather.7
  196.0 34.4 all-gather.9
  266.4 44.5 reduce-scatter.8
  313.4 44.5 reduce-scatter.6
  364.5 34.4 all-gather.11
  483.2 211.0 all-reduce.6
  696.9 43.6 reduce-scatter.10
where the time goes:
time: 801 us; the launch traced here: 796 us
  waiting for transfers between devices  426 us (53%)
  matrix products  158 us (20%)
  other arithmetic  80 us (10%)
  blocking collectives  68.8 us (9%)
  local copies, waits for them, and re-layouts  47.6 us (6%)
  between operations  14.9 us (2%)
    psum x1, waiting for transfers between devices, shards(): lax.psum(grad_qkv.astype(jnp.bfloat16), 'dp').astype(jnp.float32)  171 us
    reduce_scatter x1, waiting for transfers between devices, shards(): lax.psum_scatter(jnp.dot(activ, w_down, preferred_element_type=jnp.float3...  44.7 us
    reduce_scatter x1, waiting for transfers between devices, shards(): lax.psum_scatter(jnp.dot(attended, w_out, preferred_element_type=jnp.floa...  44.1 us
    psum x1, blocking collectives, shards(): lax.psum((jnp.stack([grad_g1, grad_g2]), jnp.stack([grad_s1, grad_s2])),...  39.5 us
    reduce_scatter x1, waiting for transfers between devices, shards(): lax.psum_scatter(summed.astype(jnp.bfloat16), 'mp', scatter_dimension=0,...  35.1 us
    all_gather x1, waiting for transfers between devices, shards(): joined2 = lax.all_gather(lowered2, 'mp', axis=0, tiled=True)  34 us
    dot_general x1, matrix products, shards(): jnp.einsum('td,fd->tf', grad_z, w_down, preferred_element_type=jnp.float32)  27.5 us
    all_gather x1, waiting for transfers between devices, shards(): lax.all_gather(lowered, 'mp', axis=0, tiled=True)  27.5 us
  transfers between devices with their start and end apart: 9, of which 9 were waited for; matrix products, arithmetic and copies ran while one was open for 10% of the time, Pallas kernels for 0%

commit v1 on v0

--- a/solution.py
+++ b/solution.py
@@ -129,10 +129,24 @@
     local_rows = tokens.shape[0]
     normed, first_back = jax.vjp(norm_rows, resid, ln_gain[0], ln_bias[0])
     lowered = normed.astype(jnp.bfloat16)
-    joined, seg_all = (
-        lax.all_gather(lowered, "mp", axis=0, tiled=True),
-        lax.all_gather(segment_ids, "mp", axis=0, tiled=True),
-    )
+
+    def test_orders(message):
+        parts_n = jax.lax.axis_size("mp")
+        views = [(to_i, (to_i + 1) % parts_n) for to_i in range(parts_n)]
+        block_list = [(to_i, (to_i - 1) % parts_n) for to_i in range(parts_n)]
+        aux, placed = ([message], [message])
+        for _ in range(parts_n // 2):
+            h_now = jax.lax.ppermute(aux[-1], "mp", views)
+            aux.append(h_now)
+        pp = 0
+        while pp < (parts_n - 1) // 2:
+            placed.append(jax.lax.ppermute(placed[-1], "mp", block_list))
+            pp += 1
+        after = jnp.concatenate([*aux[::-1], *placed[1:]], axis=0)
+        before = jnp.roll(after, (jax.lax.axis_index("mp") - parts_n // 2) * message.shape[0], 0)
+        return before
+
+    joined, seg_all = (test_orders(lowered), lax.all_gather(segment_ids, "mp", axis=0, tiled=True))
     query = (jnp.dot(joined, w_qkv[0], preferred_element_type=jnp.float32) + qv_bias[0]).astype(
         jnp.bfloat16
     )

time: 801 us -> 824 us (1.029)
  local copies, waits for them, and re-layouts: 47.6 us -> 65.7 us
    all_gather x1 -> x0, waiting for transfers between devices: 27.5 us -> none  [shards(): lax.all_gather(lowered, 'mp', axis=0, tiled=True)]
    ppermute x0 -> x3, waiting for transfers between devices: none -> 20.2 us  [the longest x2 20.2 us: test_orders(): h_now = jax.lax.ppermute(aux[-1], 'mp', views)]
    reshape x6, local copies, waits for them, and re-layouts: 15.9 us -> 24.8 us  [split_heads(): return flat.reshape(rows, LEN, flat.shape[1] // HD, HD)]
    unnamed x132 -> x143, local copies, waits for them, and re-layouts: 20.4 us -> 27.9 us
  transfers between devices with their start and end apart: 9 -> 11, of which waited for: 9 -> 9; matrix products, arithmetic and copies ran while one was open for 10% -> 10% of each run, Pallas kernels for 0% -> 0%
where the time goes in v1:
time: 824 us; the launch traced here: 816 us
  waiting for transfers between devices  423 us (51%)
  matrix products  151 us (18%)
  other arithmetic  80.2 us (10%)
  blocking collectives  75.4 us (9%)
  local copies, waits for them, and re-layouts  65.7 us (8%)
  between operations  15.2 us (2%)
    psum x1, waiting for transfers between devices, shards(): lax.psum(grad_qkv.astype(jnp.bfloat16), 'dp').astype(jnp.float32)  171 us
    reduce_scatter x1, waiting for transfers between devices, shards(): lax.psum_scatter(jnp.dot(attended, w_out, preferred_element_type=jnp.floa...  47.9 us
    reduce_scatter x1, waiting for transfers between devices, shards(): lax.psum_scatter(jnp.dot(activ, w_down, preferred_element_type=jnp.float3...  44.7 us
    psum x1, blocking collectives, shards(): lax.psum((jnp.stack([grad_g1, grad_g2]), jnp.stack([grad_s1, grad_s2])),...  39.5 us
    reduce_scatter x1, waiting for transfers between devices, shards(): lax.psum_scatter(summed.astype(jnp.bfloat16), 'mp', scatter_dimension=0,...  35.1 us
    all_gather x1, waiting for transfers between devices, shards(): joined2 = lax.all_gather(lowered2, 'mp', axis=0, tiled=True)  33.8 us
    unnamed x143, local copies, waits for them, and re-layouts  27.9 us
    dot_general x1, matrix products, shards(): jnp.einsum('td,fd->tf', grad_z, w_down, preferred_element_type=jnp.float32)  27.4 us
  transfers between devices with their start and end apart: 11, of which 9 were waited for; matrix products, arithmetic and copies ran while one was open for 10% of the time, Pallas kernels for 0%

profile of v1, /device:TPU:0, one launch (start us, length us, event | category | flops | bytes accessed | tf_op | source)
XLA Modules:
  0.0 816.3 jit_solution(717516989512918069)
XLA Ops:
  18.4 20.2 %collective-permute-done = bf16[512,1024]{1,0:T(8,128)(2,1)} collective-permute-done((bf16[512,1024]{1,0:T(8,128)(2,1)}, bf16[512,1024]{1,0:T(8,128)(2,1)}, u32[]{:S(2)}, u32[]{:S(2)}) %collective-permute-start) | collective-permute-done | bytes 1048608 | tf_op jit(solution)/shard_map/ppermute | solution.py:139
  41.1 12.8 %all-gather = s32[4,1,512]{2,1,0:T(1,128)S(1)} all-gather(s32[1,1,512]{2,1,0:T(1,128)S(1)} %bitcast.163), channel_id=1, replica_groups=mesh['dp'=8,'mp'=4] {'mp'}, dimensions={0}, use_global_device_ids=true | all-gather | bytes 10240 | tf_op jit(solution)/shard_map/all_gather | solution.py:149
  74.3 4.6 reshape.219
  78.8 4.0 copy.62
  82.9 4.4 reshape.220
  95.4 4.4 reshape.221
  99.8 4.1 copy.66
  131.6 47.9 %reduce-scatter.5.cloned.1.call-done = bf16[512,1024]{1,0:T(8,128)(2,1)} async-done(((bf16[2048,1024]{1,0:T(8,128)(2,1)}), bf16[512,1024]{1,0:T(8,128)(2,1)}) %reduce-scatter.5.cloned.1.call-update) | async-done | bytes 1048592 | tf_op jit(solution)/shard_map/reduce_scatter | solution.py:159
  185.4 33.8 %all-gather.5.cloned.1.call-done = bf16[2048,1024]{1,0:T(8,128)(2,1)} async-done(((bf16[512,1024]{1,0:T(8,128)(2,1)}), bf16[2048,1024]{1,0:T(8,128)(2,1)}) %all-gather.5.cloned.1.call-update) | async-done | bytes 4194320 | tf_op jit(solution)/shard_map/all_gather | solution.py:168
  219.2 11.4 %fusion.121 = f32[2048,1024]{1,0:T(8,128)} fusion(bf16[2048,1024]{1,0:T(8,128)(2,1)} %all-gather.5.cloned.1.call-done, bf16[1024,1024]{1,0:T(8,128)(2,1)} %param.19), kind=kOutput, calls=%fused_computation.186 | convolution fusion | flops 4294967296 | bytes 14680064 | tf_op jit(solution)/shard_map/dot_general | solution.py:169
  230.6 24.7 %all-gather.7.cloned.1.call-done = bf16[2048,1024]{1,0:T(8,128)(2,1)} async-done(((bf16[512,1024]{1,0:T(8,128)(2,1)}), bf16[2048,1024]{1,0:T(8,128)(2,1)}) %all-gather.7.cloned.1.call-update) | async-done | bytes 4194320 | tf_op jit(solution)/shard_map/all_gather | solution.py:182
  255.3 27.4 %fusion.108 = (bf16[1024]{0:T(1024)(128)(2,1)S(1)}, bf16[2048,1024]{1,0:T(8,128)(2,1)S(1)}, f32[2048,1024]{1,0:T(8,128)}) fusion(f32[2048,1024]{1,0:T(8,128)} %fusion.121, f32[1024]{0:T(1024)S(1)} %convert_element_type.188, bf16[2048,1024]{1,0:T(8,128)(2,1)} %all-gather.7.cloned.1.call-done, bf16[1024,1024]{1,0:T(8,128)(2,1)S(1)} %copy-done), kind=kOutput, calls=%fused_computation.174 | convolution fusion | flops 4450155520 | bytes 27269120 | tf_op jit(solution)/shard_map/td,fd->tf/dot_general | solution.py:185
  284.7 6.2 convolution_convert_fusion.1
  291.0 10.4 %multiply_convert_fusion.2 = bf16[2048,1024]{1,0:T(8,128)(2,1)} fusion(f32[2048,1024]{1,0:T(8,128)} %get-tuple-element.31, f32[2048,1024]{1,0:T(8,128)} %fusion.121, f32[1024]{0:T(1024)S(1)} %convert_element_type.188), kind=kLoop, calls=%fused_computation.17 | loop fusion | flops 8388608 | bytes 20975616 | tf_op jit(solution)/shard_map/convert_element_type | solution.py:170
  301.4 8.4 %convolution_convert_fusion.2 = bf16[2048,1024]{1,0:T(8,128)(2,1)} fusion(bf16[2048,1024]{1,0:T(8,128)(2,1)} %multiply_convert_fusion.2, bf16[1024,1024]{1,0:T(8,128)(2,1)S(1)} %copy-done), kind=kOutput, calls=%fused_computation.43 | convolution fusion | flops 4297064448 | bytes 10485760 | tf_op jit(solution)/shard_map/dot_general | solution.py:174
  310.4 25.2 %reduce-scatter.9.cloned.1.call-done = bf16[512,1024]{1,0:T(8,128)(2,1)} async-done(((bf16[2048,1024]{1,0:T(8,128)(2,1)}), bf16[512,1024]{1,0:T(8,128)(2,1)}) %reduce-scatter.9.cloned.1.call-update) | async-done | bytes 1048592 | tf_op jit(solution)/shard_map/reduce_scatter | solution.py:190
  338.0 44.7 %reduce-scatter.7.cloned.1.call-done = bf16[512,1024]{1,0:T(8,128)(2,1)} async-done(((bf16[2048,1024]{1,0:T(8,128)(2,1)}), bf16[512,1024]{1,0:T(8,128)(2,1)}) %reduce-scatter.7.cloned.1.call-update) | async-done | bytes 1048592 | tf_op jit(solution)/shard_map/reduce_scatter | solution.py:173
  389.1 9.5 %convolution_convert_fusion.6 = bf16[1024,1024]{1,0:T(8,128)(2,1)} fusion(bf16[2048,1024]{1,0:T(8,128)(2,1)} %all-gather.5.cloned.1.call-done, bf16[2048,1024]{1,0:T(8,128)(2,1)} %copy-done.56), kind=kOutput, calls=%fused_computation.90 | convolution fusion | flops 4296015872 | bytes 10485760 | tf_op jit(solution)/shard_map/td,tf->df/dot_general | solution.py:188
  398.6 6.0 convolution_convert_fusion.5
  404.6 19.0 %all-gather.9.cloned.1.call-done = bf16[2048,1024]{1,0:T(8,128)(2,1)} async-done(((bf16[512,1024]{1,0:T(8,128)(2,1)}), bf16[2048,1024]{1,0:T(8,128)(2,1)}) %all-gather.9.cloned.1.call-update) | async-done | bytes 4194320 | tf_op jit(solution)/shard_map/all_gather | solution.py:200
  423.6 4.4 convolution_convert_fusion.3
  435.0 5.9 fusion.51
  440.9 4.6 multiply_reduce_fusion.1
  454.2 12.4 %multiply_reduce_fusion = (f32[2,4,512]{2,1,0:T(4,128)S(1)}, f32[2,4,512,1024]{3,2,1,0:T(8,128)}) fusion(f32[2,4,512,1024]{3,2,1,0:T(8,128)} %copy-done.2, f32[2,4,512]{2,1,0:T(4,128)S(1)} %bitcast.134, bf16[2,512,4,64]{1,3,2,0:T(8,128)(2,1)} %copy.98, bf16[2,1024,4,64]{1,3,2,0:T(8,128)(2,1)S(1)} %copy-done.14), kind=kOutput, calls=%fused_computation.1 | convolution fusion | flops 549449728 | bytes 35160064 | tf_op jit(solution)/shard_map/rqhd,rkhd->rhqk/dot_general | solution.py:79
  466.7 7.7 fusion.120
  475.7 4.8 fusion.70
  480.6 8.1 multiply_convert_fusion
  517.7 23.1 %all-reduce.3 = (bf16[2,256]{1,0:T(2,128)(2,1)S(1)}, bf16[1024]{0:T(1024)(128)(2,1)S(1)}, bf16[1024]{0:T(1024)(128)(2,1)S(1)}, bf16[1024]{0:T(1024)(128)(2,1)S(1)}) all-reduce(bf16[2,256]{1,0:T(2,128)(2,1)S(1)} %pad_maximum_fusion.4, bf16[1024]{0:T(1024)(128)(2,1)S(1)} %reduce_sum.244, ...), channel_id=1, replica_groups=mesh['dp'=8,'mp'=4] {'dp'}, use_global_device_ids=true, to_apply=%region_21.22 | all-reduce | flops 3584 | bytes 14336 | tf_op jit(solution)/shard_map/psum | solution.py:228
  543.1 171.4 %all-reduce.7.cloned.1.call-done = (bf16[3,1024,256]{2,1,0:T(8,128)(2,1)}, bf16[256,1024]{1,0:T(8,128)(2,1)}, bf16[1024,1024]{1,0:T(8,128)(2,1)}, bf16[1024,1024]{1,0:T(8,128)(2,1)}) async-done(((bf16[3,1024,256]{2,1,0:T(8,128)(2,1)}, bf16[256,1024]{1,0:T(8,128)(2,1)}, bf16[1024,1024]{1,0:T(8,128)(2,1)}, bf16[1024,1024]{1,0:T(8,128)(2,1)}), (bf16[3,1024,256]{2,1,0:T(8,128)(2,1)}, ...) | async-done | bytes 6291472 | tf_op jit(solution)/shard_map/psum | solution.py:227
  725.6 35.1 %reduce-scatter.11.cloned.1.call-done = bf16[512,1024]{1,0:T(8,128)(2,1)} async-done(((bf16[2048,1024]{1,0:T(8,128)(2,1)}), bf16[512,1024]{1,0:T(8,128)(2,1)}) %reduce-scatter.11.cloned.1.call-update) | async-done | bytes 1048592 | tf_op jit(solution)/shard_map/reduce_scatter | solution.py:221
  765.3 39.5 %all-reduce.2 = (f32[2,1024]{1,0:T(2,128)}, f32[2,1024]{1,0:T(2,128)}) all-reduce(f32[2,1024]{1,0:T(2,128)S(1)} %get-tuple-element.59, f32[2,1024]{1,0:T(2,128)S(1)} %get-tuple-element.60), channel_id=1, replica_groups=mesh['dp'=8,'mp'=4] {'dp','mp'}, use_global_device_ids=true, to_apply=%region_33.34 | all-reduce | flops 4096 | bytes 32768 | tf_op jit(solution)/shard_map/psum | solution.py:236
  804.7 4.5 add_add_fusion.2
  (250 shorter events, 150.4 us)
Async XLA Ops:
  7.2 248.1 %copy-start = (bf16[1024,1024]{1,0:T(8,128)(2,1)S(1)}, bf16[1024,1024]{1,0:T(8,128)(2,1)}, u32[]{:S(2)}) copy-start(bf16[1024,1024]{1,0:T(8,128)(2,1)} %param.21) | copy-start | bytes 6291460
  7.2 33.9 %copy-start.51 = (s32[512]{0:T(512)S(1)}, s32[512]{0:T(512)}, u32[]{:S(2)}) copy-start(s32[512]{0:T(512)} %param.14) | copy-start | bytes 6148
  7.2 48.1 %copy-start.50 = (bf16[2,256]{1,0:T(2,128)(2,1)S(1)}, bf16[2,256]{1,0:T(2,128)(2,1)}, u32[]{:S(2)}) copy-start(bf16[2,256]{1,0:T(2,128)(2,1)} %param.16) | copy-start | bytes 3076
  7.2 172.2 %reduce-scatter.5.cloned.1.call-start = ((), (), s32[]{:S(2)}) async-start(), calls=%async_computation.4 | async-start | bytes 5242880 | tf_op jit(solution)/shard_map/reduce_scatter | solution.py:159
  8.8 56.4 %copy-start.42 = (f32[512]{0:T(512)}, f32[512]{0:T(512)S(1)}, u32[]{:S(2)}) copy-start(f32[512]{0:T(512)S(1)} %broadcast_multiply_fusion.1) | copy-start | bytes 6148
  10.5 30.6 %copy-start.48 = (f32[512]{0:T(512)}, f32[512]{0:T(512)S(1)}, u32[]{:S(2)}) copy-start(f32[512]{0:T(512)S(1)} %fusion.31) | copy-start | bytes 6148
  10.5 54.7 %copy-start.44 = (f32[512]{0:T(512)}, f32[512]{0:T(512)S(1)}, u32[]{:S(2)}) copy-start(f32[512]{0:T(512)S(1)} %fusion.100) | copy-start | bytes 6148
  11.3 53.9 %copy-start.37 = (f32[1,1024]{1,0:T(1,128)}, f32[1,1024]{1,0:T(1,128)S(1)}, u32[]{:S(2)}) copy-start(f32[1,1024]{1,0:T(1,128)S(1)} %get-tuple-element.43) | copy-start | bytes 12292
  14.7 46.0 %copy-start.4 = (bf16[512,1024]{1,0:T(8,128)(2,1)S(1)}, bf16[512,1024]{1,0:T(8,128)(2,1)}, u32[]{:S(2)}) copy-start(bf16[512,1024]{1,0:T(8,128)(2,1)} %param.13) | copy-start | bytes 3145732
  14.7 23.8 %collective-permute-start = (bf16[512,1024]{1,0:T(8,128)(2,1)}, bf16[512,1024]{1,0:T(8,128)(2,1)}, u32[]{:S(2)}, u32[]{:S(2)}) collective-permute-start(bf16[512,1024]{1,0:T(8,128)(2,1)} %fusion.29), channel_id=1, source_target_pairs={{0,1},{1,2},{2,3},{3,0},{4,5},{5,6},{6,7},{7,4},{8,9},{9,10},{10,1... | collective-permute-start | bytes 3145736 | tf_op jit(solution)/shard_map/ppermute | solution.py:139
  15.2 45.9 %collective-permute-start.2 = (bf16[512,1024]{1,0:T(8,128)(2,1)}, bf16[512,1024]{1,0:T(8,128)(2,1)}, u32[]{:S(2)}, u32[]{:S(2)}) collective-permute-start(bf16[512,1024]{1,0:T(8,128)(2,1)} %fusion.29), channel_id=1, source_target_pairs={{0,3},{1,0},{2,1},{3,2},{4,7},{5,4},{6,5},{7,6},{8,11},{9,8},{10,9... | collective-permute-start | bytes 3145736 | tf_op jit(solution)/shard_map/ppermute | solution.py:143
  38.6 19.5 %collective-permute-start.1 = (bf16[512,1024]{1,0:T(8,128)(2,1)}, bf16[512,1024]{1,0:T(8,128)(2,1)}, u32[]{:S(2)}, u32[]{:S(2)}) collective-permute-start(bf16[512,1024]{1,0:T(8,128)(2,1)} %collective-permute-done), channel_id=1, source_target_pairs={{0,1},{1,2},{2,3},{3,0},{4,5},{5,6},{6,7},{7,4},{8,9},{9,10},{10,1... | collective-permute-start | bytes 3145736 | tf_op jit(solution)/shard_map/ppermute | solution.py:139
  130.9 88.3 %all-gather.5.cloned.1.call-start = ((), (), s32[]{:S(2)}) async-start(), calls=%async_computation.5 | async-start | bytes 5242880 | tf_op jit(solution)/shard_map/all_gather | solution.py:168
  184.6 70.7 %all-gather.7.cloned.1.call-start = ((), (), s32[]{:S(2)}) async-start(), calls=%async_computation.7 | async-start | bytes 5242880 | tf_op jit(solution)/shard_map/all_gather | solution.py:182
  185.3 150.3 %reduce-scatter.9.cloned.1.call-start = ((), (), s32[]{:S(2)}) async-start(), calls=%async_computation.8 | async-start | bytes 5242880 | tf_op jit(solution)/shard_map/reduce_scatter | solution.py:190
  255.3 29.4 %copy-start.55 = (bf16[1024,1024]{1,0:T(8,128)(2,1)S(1)}, bf16[1024,1024]{1,0:T(8,128)(2,1)}, u32[]{:S(2)}) copy-start(bf16[1024,1024]{1,0:T(8,128)(2,1)} %param.19) | copy-start | bytes 6291460
  290.9 91.7 %reduce-scatter.7.cloned.1.call-start = ((), (), s32[]{:S(2)}) async-start(), calls=%async_computation.6 | async-start | bytes 5242880 | tf_op jit(solution)/shard_map/reduce_scatter | solution.py:173
  309.8 25.9 %copy-start.6 = (bf16[512,1024]{1,0:T(8,128)(2,1)S(1)}, bf16[512,1024]{1,0:T(8,128)(2,1)}, u32[]{:S(2)}) copy-start(bf16[512,1024]{1,0:T(8,128)(2,1)} %reduce-scatter.5.cloned.1.call-done) | copy-start | bytes 3145732
  309.8 113.8 %all-gather.9.cloned.1.call-start = ((), (), s32[]{:S(2)}) async-start(), calls=%async_computation.9 | async-start | bytes 5242880 | tf_op jit(solution)/shard_map/all_gather | solution.py:200
  337.9 49.7 %copy-start.10 = (bf16[512,1024]{1,0:T(8,128)(2,1)S(1)}, bf16[512,1024]{1,0:T(8,128)(2,1)}, u32[]{:S(2)}) copy-start(bf16[512,1024]{1,0:T(8,128)(2,1)} %param.25) | copy-start | bytes 3145732
  389.0 325.6 %all-reduce.7.cloned.1.call-start = ((), (), s32[]{:S(2)}) async-start(), calls=%async_computation.11 | async-start | bytes 12582912 | tf_op jit(solution)/shard_map/psum | solution.py:227
  398.6 25.0 %copy-start.35 = (bf16[256,1024]{1,0:T(8,128)(2,1)S(1)}, bf16[256,1024]{1,0:T(8,128)(2,1)}, u32[]{:S(2)}) copy-start(bf16[256,1024]{1,0:T(8,128)(2,1)} %param.17) | copy-start | bytes 1572868
  454.2 12.4 %copy-start.21 = (f32[2,512,4,64]{1,3,2,0:T(8,128)S(1)}, f32[2,512,4,64]{1,3,2,0:T(8,128)}, u32[]{:S(2)}) copy-start(f32[2,512,4,64]{1,3,2,0:T(8,128)} %fusion.51) | copy-start | bytes 3145732
  466.7 13.9 %slice-start = ((s8[16777216]{0:T(1024)(128)(4,1)}), s8[4194304]{0:T(1024)(128)(4,1)S(1)}, s32[]{:S(2)}) async-start(s8[16777216]{0:T(1024)(128)(4,1)} %bitcast.118), calls=%async_computation.12 | async-start | bytes 8388608
  466.7 13.9 %slice-start.1 = ((s8[16777216]{0:T(1024)(128)(4,1)}), s8[4194304]{0:T(1024)(128)(4,1)S(1)}, s32[]{:S(2)}) async-start(s8[16777216]{0:T(1024)(128)(4,1)} %bitcast.118), calls=%async_computation.13 | async-start | bytes 8388608
  466.7 13.9 %slice-start.2 = ((s8[16777216]{0:T(1024)(128)(4,1)}), s8[4194304]{0:T(1024)(128)(4,1)S(1)}, s32[]{:S(2)}) async-start(s8[16777216]{0:T(1024)(128)(4,1)} %bitcast.118), calls=%async_computation.14 | async-start | bytes 8388608
  503.3 257.4 %reduce-scatter.11.cloned.1.call-start = ((), (), s32[]{:S(2)}) async-start(), calls=%async_computation.10 | async-start | bytes 5242880 | tf_op jit(solution)/shard_map/reduce_scatter | solution.py:221
  722.6 38.1 %copy-start.38 = (f32[1,1024]{1,0:T(1,128)S(1)}, f32[1,1024]{1,0:T(1,128)}, u32[]{:S(2)}) copy-start(f32[1,1024]{1,0:T(1,128)} %copy-done.37) | copy-start | bytes 12292
  722.6 38.1 %copy-start.43 = (f32[512]{0:T(512)S(1)}, f32[512]{0:T(512)}, u32[]{:S(2)}) copy-start(f32[512]{0:T(512)} %copy-done.42) | copy-start | bytes 6148
  722.6 40.0 %copy-start.49 = (f32[512]{0:T(512)S(1)}, f32[512]{0:T(512)}, u32[]{:S(2)}) copy-start(f32[512]{0:T(512)} %copy-done.48) | copy-start | bytes 6148
  722.6 40.0 %copy-start.45 = (f32[512]{0:T(512)S(1)}, f32[512]{0:T(512)}, u32[]{:S(2)}) copy-start(f32[512]{0:T(512)} %copy-done.44) | copy-start | bytes 6148
  762.7 46.6 %copy-start.1 = (bf16[1024,1024]{1,0:T(8,128)(2,1)S(1)}, bf16[1024,1024]{1,0:T(8,128)(2,1)}, u32[]{:S(2)}) copy-start(bf16[1024,1024]{1,0:T(8,128)(2,1)} %param.21) | copy-start | bytes 6291460
  (44 other events, 159.7 us)
Sparse Core Ops, SparseCore 0:
  131.0 48.3 reduce-scatter.4
  184.7 34.4 all-gather.4
  220.8 34.4 all-gather.6
  291.0 44.5 reduce-scatter.8
  338.0 44.5 reduce-scatter.6
  389.1 34.4 all-gather.8
  503.4 211.0 all-reduce.6
  717.1 43.6 reduce-scatter.10
